TPU v7x, 32 devices: a whole 2x2x4 slice. The times are simulated.
32 devices in a mesh: dp: 8 (over z, core), seq: 4 (over y, x).
Axes of the slice: x: 2, y: 2, z: 4, core: 2. Of those that a mesh axis runs over, the one named last changes fastest.
Arguments:
- waveform: bfloat16 [32, 2560], P('dp', 'seq'), may hold values from -6 to 6
- lengths: int32 [8, 4], P('dp'), may hold values from 1 to 2560, 6400 in all within a row
- conv_one: bfloat16 [10, 512], replicated, may hold values from -2 to 2
- conv_two: bfloat16 [1536, 512], replicated, may hold values from -0.15625 to 0.15625
- gain_one: float32 [512], replicated, may hold values from 0.1 to 1.9
- shift_one: float32 [512], replicated, may hold values from -3 to 3
- gain_two: float32 [512], replicated, may hold values from 0.1 to 1.9
- shift_two: float32 [512], replicated, may hold values from -3 to 3
- cotangent: bfloat16 [32, 256, 512], P('dp', 'seq'), may hold values from -0.0625 to 0.0625
Outputs:
- features: bfloat16 [32, 256, 512], P('dp', 'seq')
- conv_one_grad: float32 [10, 512], replicated
- conv_two_grad: float32 [1536, 512], P('seq')
- norm_grads: float32 [4, 512], replicated
Inputs may be any that keep to these rules, and one draw needn't show every extreme that they name: In each row of lengths the 4 lengths sum to 6400 and the longest is exactly 2560.
All inputs are finite; a program needn't handle non-finite values.
Results may differ from a plain program's by a relative error of at most 0.0054.
Values may be sent and summed in bfloat16 or wider, within the bound.
A program may use at most 64 MiB of HBM per device.

v0:
```python
import jax
import jax.numpy as jnp
from jax import lax
from jax.sharding import PartitionSpec as P

epsilon = 1e-05
root_half = 0.7071067811865476
normal_peak = 0.3989422804014327


def passed_along(value, axis, steps):
    count = lax.axis_size(axis)
    first, last = (max(0, -steps), min(count, count - steps))
    return lax.ppermute(value, axis, [(source, source + steps) for source in range(first, last)])


def norm_forward(preact, gain_vector, offset):
    centre = preact - jnp.mean(preact, axis=-1, keepdims=True)
    inverse = lax.rsqrt(jnp.mean(centre * centre, axis=-1, keepdims=True) + epsilon)
    normed = centre * inverse
    return (normed, inverse, normed * gain_vector + offset)


def gelu_slope(values):
    return (
        0.5 * (1.0 + lax.erf(values * root_half))
        + values * jnp.exp(-0.5 * values * values) * normal_peak
    )


def norm_backward(upstream, normed, inverse, gain_vector):
    scaled = upstream * gain_vector
    return inverse * (
        scaled
        - jnp.mean(scaled, axis=-1, keepdims=True)
        - normed * jnp.mean(scaled * normed, axis=-1, keepdims=True)
    )


def on_device(
    waveform, lengths, conv_one, conv_two, gain_one, shift_one, gain_two, shift_two, cotangent
):
    clip_count, samples = waveform.shape
    frames_one = samples // 5
    frames_two = cotangent.shape[1]
    channels = conv_two.shape[1]
    position = lax.axis_index("seq")
    border = passed_along(waveform[:, :16], "seq", -1)
    extended = jnp.concatenate([waveform, border], axis=1)
    blocks = extended[:, : 5 * (frames_one + 1)].reshape(clip_count, frames_one + 1, 5)
    patch_one = jnp.concatenate([blocks[:, :-1], blocks[:, 1:]], axis=2).reshape(
        clip_count * frames_one, 10
    )
    pre_one = jnp.dot(patch_one, conv_one, preferred_element_type=jnp.float32)
    normed_one, inverse_one, output_one = norm_forward(pre_one, gain_one, shift_one)
    active_one = (
        jax.nn.gelu(output_one, approximate=False)
        .astype(jnp.bfloat16)
        .reshape(clip_count, frames_one, channels)
    )
    edge_frame = passed_along(active_one[:, :1], "seq", -1)
    widened = jnp.concatenate([active_one, edge_frame], axis=1)
    patch_two = jnp.concatenate(
        [widened[:, :frames_one].reshape(clip_count, frames_two, 2 * channels), widened[:, 2::2]],
        axis=2,
    ).reshape(clip_count * frames_two, 3 * channels)
    pre_two = jnp.dot(patch_two, conv_two, preferred_element_type=jnp.float32)
    normed_two, inverse_two, output_two = norm_forward(pre_two, gain_two, shift_two)
    lengths_row = lengths[0]
    first_frames = (lengths_row - 5) // 5
    second_frames = (first_frames - 1) // 2
    frame_index = position * frames_two + lax.broadcasted_iota(
        jnp.int32, (clip_count, frames_two), 1
    )
    validity = (
        (frame_index < second_frames[:, None])
        .astype(jnp.float32)
        .reshape(clip_count * frames_two, 1)
    )
    features = (
        (jax.nn.gelu(output_two, approximate=False) * validity)
        .astype(jnp.bfloat16)
        .reshape(clip_count, frames_two, channels)
    )
    upstream_two = (
        cotangent.reshape(clip_count * frames_two, channels).astype(jnp.float32)
        * validity
        * gelu_slope(output_two)
    )
    dpre_two = norm_backward(upstream_two, normed_two, inverse_two, gain_two).astype(jnp.bfloat16)
    dpatch_two = lax.dot_general(
        dpre_two, conv_two, (((1,), (1,)), ((), ())), preferred_element_type=jnp.float32
    ).reshape(clip_count, frames_two, 3 * channels)
    paired = dpatch_two[:, :, : 2 * channels].reshape(clip_count, frames_two, 2, channels)
    onward = dpatch_two[:, :, 2 * channels :]
    carried = jnp.concatenate([passed_along(onward[:, -1:], "seq", 1), onward[:, :-1]], axis=1)
    dact_one = jnp.stack([paired[:, :, 0] + carried, paired[:, :, 1]], axis=2).reshape(
        clip_count, frames_one, channels
    )
    upstream_one = dact_one.reshape(clip_count * frames_one, channels) * gelu_slope(output_one)
    dpre_one = norm_backward(upstream_one, normed_one, inverse_one, gain_one)
    grad_one = lax.dot_general(
        patch_one.astype(jnp.float32),
        dpre_one,
        (((0,), (0,)), ((), ())),
        precision=lax.Precision.HIGHEST,
        preferred_element_type=jnp.float32,
    )
    norm_terms = jnp.stack(
        [
            jnp.sum(upstream_one * normed_one, 0),
            jnp.sum(upstream_one, 0),
            jnp.sum(upstream_two * normed_two, 0),
            jnp.sum(upstream_two, 0),
        ]
    )
    grad_one_sum, norm_sum = lax.psum((grad_one, norm_terms), ("dp", "seq"))
    seq_share = lax.psum_scatter(
        lax.dot_general(
            patch_two, dpre_two, (((0,), (0,)), ((), ())), preferred_element_type=jnp.float32
        ),
        "seq",
        scatter_dimension=0,
        tiled=True,
    )
    grad_two = lax.psum(seq_share, "dp")
    return (features, grad_one_sum, grad_two, norm_sum)


def solution(mesh):
    in_specs = (P("dp", "seq"), P("dp", None), P(), P(), P(), P(), P(), P(), P("dp", "seq", None))
    out_specs = (P("dp", "seq", None), P(), P("seq", None), P())
    return jax.shard_map(
        on_device, mesh=mesh, in_specs=in_specs, out_specs=out_specs, check_vma=False
    )
```

profile of v0, /device:TPU:0, one launch (start us, length us, event | category | flops | bytes accessed | tf_op | source)
XLA Modules:
  0.0 152.2 jit_solution(17305733421126608220)
XLA Ops:
  7.2 0.0 copy-start
  7.2 0.0 reduce-scatter.2.cloned.1.call-start
  7.2 0.8 slice.36
  8.0 1.3 collective-permute-start
  9.3 0.7 and_select_fusion
  10.0 4.4 %collective-permute-done = bf16[4,16]{1,0:T(4,128)(2,1)S(1)} collective-permute-done((bf16[4,16]{1,0:T(4,128)(2,1)S(1)}, bf16[4,16]{1,0:T(4,128)(2,1)S(1)}, u32[]{:S(2)}, u32[]{:S(2)}) %collective-permute-start) | collective-permute-done | bytes 160 | tf_op jit(solution)/shard_map/ppermute | solution.py:14
  14.4 0.7 pad_maximum_fusion.6
  15.1 0.0 copy-start.5
  15.1 0.0 copy-start.6
  15.1 0.2 reshape.138
  15.4 0.1 copy.16
  15.5 0.1 copy.17
  15.7 1.1 fusion.49
  16.8 0.3 multiply_reduce_fusion.2
  17.1 0.0 copy-done.5
  17.1 0.0 copy-done.6
  17.1 3.0 %fusion.2 = bf16[512,512]{1,0:T(8,128)(2,1)S(1)} fusion(f32[512,512]{1,0:T(8,128)S(1)} %get-tuple-element.22, f32[512]{0:T(512)S(1)} %copy-done.6, f32[512]{0:T(512)S(1)} %copy-done.5, f32[512]{0:T(512)S(1)} %add_rsqrt_fusion, f32[512]{0:T(512)S(1)} %broadcast_multiply_fusion.2), kind=kLoop, calls=%fused_computation.4 | loop fusion | flops 18087936 | bytes 1581056 | tf_op jit(solution)/shard_map/convert_element_type | solution.py:58
  20.1 1.3 collective-permute-start.1
  21.4 0.1 compare_convert_fusion
  21.5 0.1 reshape.144
  21.6 1.0 concatenate.27
  22.6 4.0 %collective-permute-done.1 = bf16[4,1,512]{2,1,0:T(2,128)(2,1)S(1)} collective-permute-done((bf16[4,1,512]{2,1,0:T(2,128)(2,1)S(1)}, bf16[4,1,512]{2,1,0:T(2,128)(2,1)S(1)}, u32[]{:S(2)}, u32[]{:S(2)}) %collective-permute-start.1) | collective-permute-done | bytes 4128 | tf_op jit(solution)/shard_map/ppermute | solution.py:14
  26.6 0.9 pad_maximum_fusion.2
  27.4 2.1 %slice.41 = bf16[4,64,512]{2,1,0:T(8,128)(2,1)S(1)} slice(bf16[4,129,512]{2,1,0:T(8,128)(2,1)} %pad_maximum_fusion.2), slice={[0:4:1], [2:129:2], [0:512:1]} | slice | bytes 524288 | tf_op jit(solution)/shard_map/slice | solution.py:64
  29.5 0.0 copy-done
  29.6 0.0 copy-start.3
  29.6 0.0 copy-start.4
  29.6 0.0 copy-start.7
  29.6 1.7 %fusion.50 = (f32[256]{0:T(256)S(1)}, f32[256,512]{1,0:T(8,128)S(1)}) fusion(bf16[1536,512]{1,0:T(8,128)(2,1)S(1)} %copy-done, bf16[256,512]{1,0:T(8,128)(2,1)S(1)} %bitcast.39, bf16[256,1024]{1,0:T(8,128)(2,1)} %concatenate.27), kind=kOutput, calls=%fused_computation.105 | convolution fusion | flops 404356864 | bytes 2884608 | tf_op jit(solution)/shard_map/dot_general | solution.py:67
  31.3 0.0 copy-start.2
  31.3 0.2 multiply_reduce_fusion.6
  31.6 0.0 copy-done.3
  31.6 0.0 copy-done.4
  31.6 0.0 copy-done.7
  31.6 2.5 %multiply_reduce_fusion.4 = (f32[512]{0:T(512)S(1)}, f32[256]{0:T(256)S(1)}, f32[256]{0:T(256)S(1)}, f32[512]{0:T(512)S(1)}, f32[256,512]{1,0:T(8,128)S(1)}, /*index=5*/bf16[256,512]{1,0:T(8,128)(2,1)}) fusion(f32[256,512]{1,0:T(8,128)S(1)} %get-tuple-element.24, f32[256]{0:T(256)S(1)} %add_rsqrt_fusion.1, f32[256]{0:T(256)S(1)} %broadcast_multiply_fusion.5, ...), kind=kLoop, calls=%fused_computation.54 | loop fusion | flops 11532800 | bytes 1586176 | tf_op jit(solution)/shard_map/reduce_sum | solution.py:113
  34.1 0.0 copy-start.1
  34.1 0.8 copy-done.1
  34.9 0.0 copy-done.2
  34.9 2.4 %fusion.42 = f32[1536,512]{1,0:T(8,128)} fusion(bf16[256,512]{1,0:T(8,128)(2,1)S(1)} %bitcast.40, bf16[256,1024]{1,0:T(8,128)(2,1)S(1)} %copy-done.2, f32[256,512]{1,0:T(8,128)S(1)} %get-tuple-element.15, f32[256,512]{1,0:T(8,128)S(1)} %get-tuple-element.24, f32[256]{0:T(256)S(1)} %get-tuple-element.25, f32[256]{0:T(256)S(1)} %get-tuple-element.26, ...), kind=kOutput, calls=%fused_computation.79 | convolution fusion | flops 405274624 | bytes 4986880 | tf_op jit(solution)/shard_map/dot_general | solution.py:119
  37.3 0.0 reduce-scatter.2.cloned.1.call-update
  37.4 0.0 all-reduce.3.cloned.1.call-start
  37.4 1.7 %fusion.51 = f32[256,1536]{1,0:T(8,128)S(1)} fusion(bf16[1536,512]{1,0:T(8,128)(2,1)S(1)} %copy-done, f32[256,512]{1,0:T(8,128)} %copy-done.1, f32[256,512]{1,0:T(8,128)S(1)} %get-tuple-element.24, f32[256]{0:T(256)S(1)} %get-tuple-element.25, f32[256]{0:T(256)S(1)} %get-tuple-element.26, f32[512]{0:T(512)S(1)} %copy-done.4, f32[256]{0:T(256)S(1)} %add_rsqrt_fusion.1, ...), kind=kOutput, calls=%fused_computation.106 | convolution fusion | flops 403701760 | bytes 4200448 | tf_op jit(solution)/shard_map/dot_general | solution.py:91
  39.2 5.0 %collective-permute-start.2 = (f32[4,1,512]{2,1,0:T(1,128)S(1)}, f32[4,1,512]{2,1,0:T(1,128)S(1)}, u32[]{:S(2)}, u32[]{:S(2)}) collective-permute-start(f32[4,1,512]{2,1,0:T(1,128)S(1)} %slice.52), channel_id=1, source_target_pairs={{0,1},{1,2},{2,3},{4,5},{5,6},{6,7},{8,9},{9,10},{10,11},{12,13},{... | collective-permute-start | bytes 24584 | tf_op jit(solution)/shard_map/ppermute | solution.py:14
  44.2 1.1 slice.50
  45.3 3.3 %reshape.143 = f32[4,64,2,512]{3,2,1,0:T(2,128)} reshape(f32[4,64,1024]{2,1,0:T(8,128)} %slice.50) | data formatting | bytes 2097152 | tf_op jit(solution)/shard_map/reshape | solution.py:94
  48.6 0.5 copy.18
  49.1 0.0 collective-permute-done.2
  49.1 2.8 %slice_add_fusion = (f32[4,64,1,512]{3,2,1,0:T(1,128)S(1)}, f32[4,64,1,512]{3,2,1,0:T(1,128)S(1)}) fusion(f32[4,64,2,512]{3,2,1,0:T(2,128)} %reshape.143, f32[4,63,1,512]{3,2,1,0:T(1,128)S(1)} %copy.18, f32[4,1,1,512]{3,2,1,0:T(1,128)S(1)} %bitcast.45), kind=kLoop, calls=%fused_computation.52 | loop fusion | flops 262144 | bytes 2621440 | tf_op jit(solution)/shard_map/add | solution.py:97
  52.0 1.9 %pad_maximum_fusion = f32[4,64,2,512]{3,2,1,0:T(2,128)} fusion(f32[4,64,1,512]{3,2,1,0:T(1,128)S(1)} %get-tuple-element.17, f32[4,64,1,512]{3,2,1,0:T(1,128)S(1)} %get-tuple-element.16), kind=kLoop, calls=%fused_computation.10 | loop fusion | flops 262144 | bytes 2097152 | tf_op jit(solution)/shard_map/stack | solution.py:97
  53.9 2.9 %reshape_reshape.4 = f32[512,512]{1,0:T(8,128)} reshape(f32[4,64,2,512]{3,2,1,0:T(2,128)} %pad_maximum_fusion) | data formatting | bytes 2097152 | tf_op jit(solution)/shard_map/reshape;reshape | solution.py:100
  56.8 3.0 %multiply_reduce_fusion = (f32[512]{0:T(512)S(1)}, f32[512]{0:T(512)S(1)}, f32[512]{0:T(512)S(1)}, f32[512]{0:T(512)S(1)}, f32[512,512]{1,0:T(8,128)}) fusion(f32[512,512]{1,0:T(8,128)S(1)} %get-tuple-element.22, f32[512]{0:T(512)S(1)} %add_rsqrt_fusion, f32[512]{0:T(512)S(1)} %broadcast_multiply_fusion.2, f32[512]{0:T(512)S(1)} %copy-done.5, ...), kind=kLoop, calls=%fused_computation.11 | loop fusion | flops 5240832 | bytes 3162112 | tf_op jit(solution)/shard_map/reduce_sum | solution.py:111
  59.9 23.3 %reduce-scatter.2.cloned.1.call-done = f32[384,512]{1,0:T(8,128)} async-done(((f32[1536,512]{1,0:T(8,128)}), f32[384,512]{1,0:T(8,128)}) %reduce-scatter.2.cloned.1.call-update) | async-done | bytes 786448 | tf_op jit(solution)/shard_map/reduce_scatter | solution.py:118
  83.1 0.0 all-reduce.3.cloned.1.call-update
  83.2 2.0 %fusion.8 = f32[10,512]{1,0:T(8,128)S(1)} fusion(bf16[512,10]{0,1:T(8,128)(2,1)S(1)} %bitcast.43, f32[512,512]{1,0:T(8,128)} %get-tuple-element.14, f32[512,512]{1,0:T(8,128)S(1)} %get-tuple-element.22, f32[512]{0:T(512)S(1)} %broadcast_multiply_fusion, f32[512]{0:T(512)S(1)} %broadcast_multiply_fusion.1, f32[512]{0:T(512)S(1)} %copy-done.5, ...), kind=kOutput, calls=%fused_computation.12 | convolution fusion | flops 33292288 | bytes 2138112 | tf_op jit(solution)/shard_map/dot_general | solution.py:102
  85.2 40.2 %all-reduce = (f32[10,512]{1,0:T(8,128)}, f32[4,512]{1,0:T(4,128)}) all-reduce(f32[10,512]{1,0:T(8,128)S(1)} %fusion.8, f32[4,512]{1,0:T(4,128)S(1)} %pad_maximum_fusion.5), channel_id=1, replica_groups=mesh['dp'=8,'seq'=4] {'dp','seq'}, use_global_device_ids=true, to_apply=%region_8.9 | all-reduce | flops 7168 | bytes 57344 | tf_op jit(solution)/shard_map/psum | solution.py:117
  125.4 17.9 %all-reduce.3.cloned.1.call-done = f32[384,512]{1,0:T(8,128)} async-done(((f32[384,512]{1,0:T(8,128)}), f32[384,512]{1,0:T(8,128)}) %all-reduce.3.cloned.1.call-update) | async-done | bytes 786448 | tf_op jit(solution)/shard_map/psum | solution.py:126
  143.3 2.1 %copy.21 = f32[384,512]{1,0:T(8,128)} copy(f32[384,512]{1,0:T(8,128)} %all-reduce.3.cloned.1.call-done) | data formatting | bytes 1572864
  (16 shorter events, 0.2 us)
Async XLA Ops:
  7.2 22.4 %copy-start = (bf16[1536,512]{1,0:T(8,128)(2,1)S(1)}, bf16[1536,512]{1,0:T(8,128)(2,1)}, u32[]{:S(2)}) copy-start(bf16[1536,512]{1,0:T(8,128)(2,1)} %param.12) | copy-start | bytes 4718596
  7.2 76.0 %reduce-scatter.2.cloned.1.call-start = ((), (), s32[]{:S(2)}) async-start(), calls=%async_computation.1 | async-start | bytes 3932160 | tf_op jit(solution)/shard_map/reduce_scatter | solution.py:118
  8.0 6.4 %collective-permute-start = (bf16[4,16]{1,0:T(4,128)(2,1)S(1)}, bf16[4,16]{1,0:T(4,128)(2,1)S(1)}, u32[]{:S(2)}, u32[]{:S(2)}) collective-permute-start(bf16[4,16]{1,0:T(4,128)(2,1)S(1)} %slice.36), channel_id=1, source_target_pairs={{1,0},{2,1},{3,2},{5,4},{6,5},{7,6},{9,8},{10,9},{11,10},{13,12},{... | collective-permute-start | bytes 392 | tf_op jit(solution)/shard_map/ppermute | solution.py:14
  15.1 2.0 %copy-start.5 = (f32[512]{0:T(512)S(1)}, f32[512]{0:T(512)}, u32[]{:S(2)}) copy-start(f32[512]{0:T(512)} %param.13) | copy-start | bytes 6148
  15.1 2.0 %copy-start.6 = (f32[512]{0:T(512)S(1)}, f32[512]{0:T(512)}, u32[]{:S(2)}) copy-start(f32[512]{0:T(512)} %param.14) | copy-start | bytes 6148
  20.1 6.4 %collective-permute-start.1 = (bf16[4,1,512]{2,1,0:T(2,128)(2,1)S(1)}, bf16[4,1,512]{2,1,0:T(2,128)(2,1)S(1)}, u32[]{:S(2)}, u32[]{:S(2)}) collective-permute-start(bf16[4,1,512]{2,1,0:T(2,128)(2,1)S(1)} %slice.49), channel_id=1, source_target_pairs={{1,0},{2,1},{3,2},{5,4},{6,5},{7,6},{9,8},{10,9},{11,10},{13,12},{... | collective-permute-start | bytes 12296 | tf_op jit(solution)/shard_map/ppermute | solution.py:14
  29.6 2.0 %copy-start.3 = (bf16[4,64,512]{2,1,0:T(8,128)(2,1)S(1)}, bf16[4,64,512]{2,1,0:T(8,128)(2,1)}, u32[]{:S(2)}) copy-start(bf16[4,64,512]{2,1,0:T(8,128)(2,1)} %param.17) | copy-start | bytes 786436
  29.6 2.0 %copy-start.4 = (f32[512]{0:T(512)S(1)}, f32[512]{0:T(512)}, u32[]{:S(2)}) copy-start(f32[512]{0:T(512)} %param.15) | copy-start | bytes 6148
  29.6 2.0 %copy-start.7 = (f32[512]{0:T(512)S(1)}, f32[512]{0:T(512)}, u32[]{:S(2)}) copy-start(f32[512]{0:T(512)} %param.16) | copy-start | bytes 6148
  31.3 3.6 %copy-start.2 = (bf16[256,1024]{1,0:T(8,128)(2,1)S(1)}, bf16[256,1024]{1,0:T(8,128)(2,1)}, u32[]{:S(2)}) copy-start(bf16[256,1024]{1,0:T(8,128)(2,1)} %concatenate.27) | copy-start | bytes 1572868
  34.1 0.8 copy-start.1
  37.4 105.9 %all-reduce.3.cloned.1.call-start = ((), (), s32[]{:S(2)}) async-start(), calls=%async_computation.2 | async-start | bytes 1572864 | tf_op jit(solution)/shard_map/psum | solution.py:126
  39.2 10.0 %collective-permute-start.2 = (f32[4,1,512]{2,1,0:T(1,128)S(1)}, f32[4,1,512]{2,1,0:T(1,128)S(1)}, u32[]{:S(2)}, u32[]{:S(2)}) collective-permute-start(f32[4,1,512]{2,1,0:T(1,128)S(1)} %slice.52), channel_id=1, source_target_pairs={{0,1},{1,2},{2,3},{4,5},{5,6},{6,7},{8,9},{9,10},{10,11},{12,13},{... | collective-permute-start | bytes 24584 | tf_op jit(solution)/shard_map/ppermute | solution.py:14
Sparse Core Ops, SparseCore 0:
  37.5 45.6 reduce-scatter.1
  85.5 57.7 all-reduce.2
where the time goes:
time: 153 us; the launch traced here: 152 us
  waiting for transfers between devices  49.6 us (32%)
  blocking collectives  40.2 us (26%)
  other arithmetic  16.1 us (11%)
  local copies, waits for them, and re-layouts  15.2 us (10%)
  between operations  14.3 us (9%)
  matrix products  8.97 us (6%)
  starting transfers between devices  7.65 us (5%)
    psum x1, blocking collectives, on_device(): grad_one_sum, norm_sum = lax.psum((grad_one, norm_terms), ('dp', 'seq'))  40.2 us
    reduce_scatter x1, waiting for transfers between devices, on_device(): lax.psum_scatter(lax.dot_general(patch_two, dpre_two, (((0,), (0,)), ((),...  23.3 us
    psum x1, waiting for transfers between devices, on_device(): grad_two = lax.psum(seq_share, 'dp')  17.9 us
    ppermute x3, waiting for transfers between devices, passed_along(): lax.ppermute(value, axis, [(source, source + steps) for source in range(f...  8.45 us
    ppermute x3, starting transfers between devices, passed_along(): lax.ppermute(value, axis, [(source, source + steps) for source in range(f...  7.57 us
    reshape x1, local copies, waits for them, and re-layouts, on_device(): dpatch_two[:, :, :2 * channels].reshape(clip_count, frames_two, 2, channels)  3.32 us
  transfers between devices with their start and end apart: 5, of which 4 were waited for; matrix products, arithmetic and copies ran while one was open for 14% of the time, Pallas kernels for 0%

commit v1 on v0

--- a/solution.py
+++ b/solution.py
@@ -123,7 +123,9 @@
         scatter_dimension=0,
         tiled=True,
     )
-    grad_two = lax.psum(seq_share, "dp")
+    grad_two = seq_share
+    for hop in (1, 2, 4):
+        grad_two = grad_two + lax.ppermute(grad_two, "dp", [(dev, dev ^ hop) for dev in range(8)])
     return (features, grad_one_sum, grad_two, norm_sum)
 
 

time: 153 us -> 179 us (1.17)
  blocking collectives: 40.2 us -> 55.2 us
  waiting for transfers between devices: 49.6 us -> 55.7 us
  other arithmetic: 16.1 us -> 20 us
  starting transfers between devices: 7.65 us -> 10.1 us
    reduce_scatter x1, waiting for transfers between devices: 23.3 us -> 45.8 us  [on_device(): lax.psum_scatter(lax.dot_general(patch_two, dpre_two, (((0,), (0,)), ((),...]
    psum x1 -> x0, waiting for transfers between devices: 17.9 us -> none  [on_device(): grad_two = lax.psum(seq_share, 'dp')]
    psum x1, blocking collectives: 40.2 us -> 55.2 us  [on_device(): grad_one_sum, norm_sum = lax.psum((grad_one, norm_terms), ('dp', 'seq'))]
    add x0 -> x3, other arithmetic: none -> 4.45 us  [on_device(): grad_two + lax.ppermute(grad_two, 'dp', [(dev, dev ^ hop) for dev in rang...]
    ppermute x0 -> x3, starting transfers between devices: none -> 3.92 us  [on_device(): lax.ppermute(grad_two, 'dp', [(dev, dev ^ hop) for dev in range(8)])]
    unnamed x19 -> x20, local copies, waits for them, and re-layouts: 2.9 us -> 0.85 us
    concatenate x2, local copies, waits for them, and re-layouts: 0.57 us -> 2.4 us  [on_device(): jnp.concatenate([passed_along(onward[:, -1:], 'seq', 1), onward[:, :-1]],...]
  transfers between devices with their start and end apart: 5 -> 7, of which waited for: 4 -> 4; matrix products, arithmetic and copies ran while one was open for 14% -> 12% of each run, Pallas kernels for 0% -> 0%
where the time goes in v1:
time: 179 us; the launch traced here: 178 us
  waiting for transfers between devices  55.7 us (31%)
  blocking collectives  55.2 us (31%)
  other arithmetic  20 us (11%)
  local copies, waits for them, and re-layouts  14.9 us (8%)
  between operations  14.3 us (8%)
  starting transfers between devices  10.1 us (6%)
  matrix products  7.84 us (4%)
    psum x1, blocking collectives, on_device(): grad_one_sum, norm_sum = lax.psum((grad_one, norm_terms), ('dp', 'seq'))  55.2 us
    reduce_scatter x1, waiting for transfers between devices, on_device(): lax.psum_scatter(lax.dot_general(patch_two, dpre_two, (((0,), (0,)), ((),...  45.8 us
    ppermute x3, waiting for transfers between devices, passed_along(): lax.ppermute(value, axis, [(source, source + steps) for source in range(f...  8.45 us
    ppermute x3, starting transfers between devices, passed_along(): lax.ppermute(value, axis, [(source, source + steps) for source in range(f...  6.14 us
    add x3, other arithmetic, on_device(): grad_two + lax.ppermute(grad_two, 'dp', [(dev, dev ^ hop) for dev in rang...  4.45 us
    ppermute x3, starting transfers between devices, on_device(): lax.ppermute(grad_two, 'dp', [(dev, dev ^ hop) for dev in range(8)])  3.92 us
  transfers between devices with their start and end apart: 7, of which 4 were waited for; matrix products, arithmetic and copies ran while one was open for 12% of the time, Pallas kernels for 0%

profile of v1, /device:TPU:0, one launch (start us, length us, event | category | flops | bytes accessed | tf_op | source)
XLA Modules:
  0.0 178.0 jit_solution(13968397889444541970)
XLA Ops:
  7.2 0.0 copy-start
  7.2 0.0 reduce-scatter.2.cloned.1.call-start
  7.2 0.8 slice.36
  8.0 1.3 collective-permute-start
  9.3 0.7 and_select_fusion
  10.0 4.4 %collective-permute-done = bf16[4,16]{1,0:T(4,128)(2,1)S(1)} collective-permute-done((bf16[4,16]{1,0:T(4,128)(2,1)S(1)}, bf16[4,16]{1,0:T(4,128)(2,1)S(1)}, u32[]{:S(2)}, u32[]{:S(2)}) %collective-permute-start) | collective-permute-done | bytes 160 | tf_op jit(solution)/shard_map/ppermute | solution.py:14
  14.4 0.7 pad_maximum_fusion.6
  15.1 0.0 copy-start.6
  15.1 0.0 copy-start.7
  15.1 0.2 reshape.138
  15.4 0.1 copy.16
  15.5 0.1 copy.17
  15.7 1.1 fusion.49
  16.8 0.3 multiply_reduce_fusion.2
  17.1 0.0 copy-done.6
  17.1 0.0 copy-done.7
  17.1 3.0 %fusion.2 = bf16[512,512]{1,0:T(8,128)(2,1)S(1)} fusion(f32[512,512]{1,0:T(8,128)S(1)} %get-tuple-element.22, f32[512]{0:T(512)S(1)} %copy-done.7, f32[512]{0:T(512)S(1)} %copy-done.6, f32[512]{0:T(512)S(1)} %add_rsqrt_fusion, f32[512]{0:T(512)S(1)} %broadcast_multiply_fusion.2), kind=kLoop, calls=%fused_computation.4 | loop fusion | flops 18087936 | bytes 1581056 | tf_op jit(solution)/shard_map/convert_element_type | solution.py:58
  20.1 1.3 collective-permute-start.1
  21.4 0.1 compare_convert_fusion
  21.5 0.1 reshape.144
  21.6 1.0 concatenate.27
  22.6 4.0 %collective-permute-done.1 = bf16[4,1,512]{2,1,0:T(2,128)(2,1)S(1)} collective-permute-done((bf16[4,1,512]{2,1,0:T(2,128)(2,1)S(1)}, bf16[4,1,512]{2,1,0:T(2,128)(2,1)S(1)}, u32[]{:S(2)}, u32[]{:S(2)}) %collective-permute-start.1) | collective-permute-done | bytes 4128 | tf_op jit(solution)/shard_map/ppermute | solution.py:14
  26.6 0.9 pad_maximum_fusion.2
  27.4 2.1 %slice.41 = bf16[4,64,512]{2,1,0:T(8,128)(2,1)S(1)} slice(bf16[4,129,512]{2,1,0:T(8,128)(2,1)} %pad_maximum_fusion.2), slice={[0:4:1], [2:129:2], [0:512:1]} | slice | bytes 524288 | tf_op jit(solution)/shard_map/slice | solution.py:64
  29.5 0.0 copy-done
  29.6 0.0 copy-start.4
  29.6 0.0 copy-start.5
  29.6 0.0 copy-start.8
  29.6 1.7 fusion.50
  31.3 0.0 copy-start.2
  31.3 0.2 multiply_reduce_fusion.6
  31.6 0.0 copy-done.4
  31.6 0.0 copy-done.5
  31.6 0.0 copy-done.8
  31.6 2.5 %multiply_reduce_fusion.4 = (f32[512]{0:T(512)S(1)}, f32[256]{0:T(256)S(1)}, f32[256]{0:T(256)S(1)}, f32[512]{0:T(512)S(1)}, f32[256,512]{1,0:T(8,128)S(1)}, /*index=5*/bf16[256,512]{1,0:T(8,128)(2,1)}) fusion(f32[256,512]{1,0:T(8,128)S(1)} %get-tuple-element.24, f32[256]{0:T(256)S(1)} %add_rsqrt_fusion.1, f32[256]{0:T(256)S(1)} %broadcast_multiply_fusion.5, ...), kind=kLoop, calls=%fused_computation.54 | loop fusion | flops 11532800 | bytes 1586176 | tf_op jit(solution)/shard_map/reduce_sum | solution.py:113
  34.1 0.0 copy-start.1
  34.1 0.8 copy-done.1
  34.9 0.0 copy-done.2
  34.9 2.4 %fusion.42 = f32[1536,512]{1,0:T(8,128)} fusion(bf16[256,512]{1,0:T(8,128)(2,1)S(1)} %bitcast.40, bf16[256,1024]{1,0:T(8,128)(2,1)S(1)} %copy-done.2, f32[256,512]{1,0:T(8,128)S(1)} %get-tuple-element.15, f32[256,512]{1,0:T(8,128)S(1)} %get-tuple-element.24, f32[256]{0:T(256)S(1)} %get-tuple-element.25, f32[256]{0:T(256)S(1)} %get-tuple-element.26, ...), kind=kOutput, calls=%fused_computation.79 | convolution fusion | flops 405274624 | bytes 4986880 | tf_op jit(solution)/shard_map/dot_general | solution.py:119
  37.3 0.0 reduce-scatter.2.cloned.1.call-update
  37.4 45.8 %reduce-scatter.2.cloned.1.call-done = f32[384,512]{1,0:T(8,128)} async-done(((f32[1536,512]{1,0:T(8,128)}), f32[384,512]{1,0:T(8,128)}) %reduce-scatter.2.cloned.1.call-update) | async-done | bytes 786448 | tf_op jit(solution)/shard_map/reduce_scatter | solution.py:118
  83.1 0.0 collective-permute-start.3
  83.1 1.8 %fusion.51 = f32[256,1536]{1,0:T(8,128)S(1)} fusion(bf16[1536,512]{1,0:T(8,128)(2,1)S(1)} %copy-done, f32[256,512]{1,0:T(8,128)} %copy-done.1, f32[256,512]{1,0:T(8,128)S(1)} %get-tuple-element.24, f32[256]{0:T(256)S(1)} %get-tuple-element.25, f32[256]{0:T(256)S(1)} %get-tuple-element.26, f32[512]{0:T(512)S(1)} %copy-done.5, f32[256]{0:T(256)S(1)} %add_rsqrt_fusion.1, ...), kind=kOutput, calls=%fused_computation.106 | convolution fusion | flops 403701760 | bytes 4200448 | tf_op jit(solution)/shard_map/dot_general | solution.py:91
  85.0 3.6 %collective-permute-start.2 = (f32[4,1,512]{2,1,0:T(1,128)S(1)}, f32[4,1,512]{2,1,0:T(1,128)S(1)}, u32[]{:S(2)}, u32[]{:S(2)}) collective-permute-start(f32[4,1,512]{2,1,0:T(1,128)S(1)} %slice.52), channel_id=1, source_target_pairs={{0,1},{1,2},{2,3},{4,5},{5,6},{6,7},{8,9},{9,10},{10,11},{12,13},{... | collective-permute-start | bytes 24584 | tf_op jit(solution)/shard_map/ppermute | solution.py:14
  88.5 0.0 collective-permute-done.3
  88.5 0.0 copy-done.3
  88.5 0.1 add.112
  88.7 1.5 collective-permute-start.4
  90.2 0.8 slice_bitcast_fusion
  91.1 1.1 slice.50
  92.1 3.1 %reshape.143 = f32[4,64,2,512]{3,2,1,0:T(2,128)} reshape(f32[4,64,1024]{2,1,0:T(8,128)} %slice.50) | data formatting | bytes 2097152 | tf_op jit(solution)/shard_map/reshape | solution.py:94
  95.3 1.6 copy.18
  96.9 0.0 collective-permute-done.2
  96.9 3.0 %slice_add_fusion = (f32[4,64,1,512]{3,2,1,0:T(1,128)S(1)}, f32[4,64,1,512]{3,2,1,0:T(1,128)S(1)}) fusion(f32[4,64,2,512]{3,2,1,0:T(2,128)} %reshape.143, f32[4,63,1,512]{3,2,1,0:T(1,128)S(1)} %copy.18, f32[4,1,1,512]{3,2,1,0:T(1,128)S(1)} %bitcast.45), kind=kLoop, calls=%fused_computation.52 | loop fusion | flops 262144 | bytes 2621440 | tf_op jit(solution)/shard_map/add | solution.py:97
  99.8 1.9 %pad_maximum_fusion = f32[4,64,2,512]{3,2,1,0:T(2,128)} fusion(f32[4,64,1,512]{3,2,1,0:T(1,128)S(1)} %get-tuple-element.17, f32[4,64,1,512]{3,2,1,0:T(1,128)S(1)} %get-tuple-element.16), kind=kLoop, calls=%fused_computation.10 | loop fusion | flops 262144 | bytes 2097152 | tf_op jit(solution)/shard_map/stack | solution.py:97
  101.8 3.0 %reshape_reshape.4 = f32[512,512]{1,0:T(8,128)} reshape(f32[4,64,2,512]{3,2,1,0:T(2,128)} %pad_maximum_fusion) | data formatting | bytes 2097152 | tf_op jit(solution)/shard_map/reshape;reshape | solution.py:100
  104.7 2.3 %multiply_reduce_fusion = (f32[512]{0:T(512)S(1)}, f32[512]{0:T(512)S(1)}, f32[512]{0:T(512)S(1)}, f32[512]{0:T(512)S(1)}, f32[512,512]{1,0:T(8,128)S(1)}) fusion(f32[512,512]{1,0:T(8,128)S(1)} %get-tuple-element.22, f32[512]{0:T(512)S(1)} %add_rsqrt_fusion, f32[512]{0:T(512)S(1)} %broadcast_multiply_fusion.2, f32[512]{0:T(512)S(1)} %copy-done.6, ...), kind=kLoop, calls=%fused_computation.11 | loop fusion | flops 5240832 | bytes 3162112 | tf_op jit(solution)/shard_map/reduce_sum | solution.py:111
  107.0 1.4 collective-permute-done.4
  108.5 2.2 %add.113 = f32[384,512]{1,0:T(8,128)} add(f32[384,512]{1,0:T(8,128)S(1)} %add.112, f32[384,512]{1,0:T(8,128)} %collective-permute-done.4) | non-fusion elementwise | flops 196608 | bytes 2359296 | tf_op jit(solution)/shard_map/add | solution.py:128
  110.6 2.4 %collective-permute-start.5 = (f32[384,512]{1,0:T(8,128)}, f32[384,512]{1,0:T(8,128)S(1)}, u32[]{:S(2)}, u32[]{:S(2)}) collective-permute-start(f32[384,512]{1,0:T(8,128)} %add.113), channel_id=1, source_target_pairs={{0,16},{4,20},{8,24},{12,28},{16,0},{20,4},{24,8},{28,12},{1,17},{... | collective-permute-start | bytes 2359304 | tf_op jit(solution)/shard_map/ppermute | solution.py:128
  113.1 0.8 fusion.8
  113.8 55.2 %all-reduce = (f32[10,512]{1,0:T(8,128)}, f32[4,512]{1,0:T(4,128)}) all-reduce(f32[10,512]{1,0:T(8,128)S(1)} %fusion.8, f32[4,512]{1,0:T(4,128)S(1)} %pad_maximum_fusion.5), channel_id=1, replica_groups=mesh['dp'=8,'seq'=4] {'dp','seq'}, use_global_device_ids=true, to_apply=%region_8.9 | all-reduce | flops 7168 | bytes 57344 | tf_op jit(solution)/shard_map/psum | solution.py:117
  169.0 0.0 collective-permute-done.5
  169.0 2.2 %add.114 = f32[384,512]{1,0:T(8,128)} add(f32[384,512]{1,0:T(8,128)} %add.113, f32[384,512]{1,0:T(8,128)S(1)} %collective-permute-done.5) | non-fusion elementwise | flops 196608 | bytes 2359296 | tf_op jit(solution)/shard_map/add | solution.py:128
  (16 shorter events, 0.2 us)
Async XLA Ops:
  7.2 22.4 %copy-start = (bf16[1536,512]{1,0:T(8,128)(2,1)S(1)}, bf16[1536,512]{1,0:T(8,128)(2,1)}, u32[]{:S(2)}) copy-start(bf16[1536,512]{1,0:T(8,128)(2,1)} %param.12) | copy-start | bytes 4718596
  7.2 76.0 %reduce-scatter.2.cloned.1.call-start = ((), (), s32[]{:S(2)}) async-start(), calls=%async_computation.1 | async-start | bytes 3932160 | tf_op jit(solution)/shard_map/reduce_scatter | solution.py:118
  8.0 6.4 %collective-permute-start = (bf16[4,16]{1,0:T(4,128)(2,1)S(1)}, bf16[4,16]{1,0:T(4,128)(2,1)S(1)}, u32[]{:S(2)}, u32[]{:S(2)}) collective-permute-start(bf16[4,16]{1,0:T(4,128)(2,1)S(1)} %slice.36), channel_id=1, source_target_pairs={{1,0},{2,1},{3,2},{5,4},{6,5},{7,6},{9,8},{10,9},{11,10},{13,12},{... | collective-permute-start | bytes 392 | tf_op jit(solution)/shard_map/ppermute | solution.py:14
  15.1 2.0 %copy-start.6 = (f32[512]{0:T(512)S(1)}, f32[512]{0:T(512)}, u32[]{:S(2)}) copy-start(f32[512]{0:T(512)} %param.13) | copy-start | bytes 6148
  15.1 2.0 %copy-start.7 = (f32[512]{0:T(512)S(1)}, f32[512]{0:T(512)}, u32[]{:S(2)}) copy-start(f32[512]{0:T(512)} %param.14) | copy-start | bytes 6148
  20.1 6.4 %collective-permute-start.1 = (bf16[4,1,512]{2,1,0:T(2,128)(2,1)S(1)}, bf16[4,1,512]{2,1,0:T(2,128)(2,1)S(1)}, u32[]{:S(2)}, u32[]{:S(2)}) collective-permute-start(bf16[4,1,512]{2,1,0:T(2,128)(2,1)S(1)} %slice.49), channel_id=1, source_target_pairs={{1,0},{2,1},{3,2},{5,4},{6,5},{7,6},{9,8},{10,9},{11,10},{13,12},{... | collective-permute-start | bytes 12296 | tf_op jit(solution)/shard_map/ppermute | solution.py:14
  29.6 2.0 %copy-start.4 = (bf16[4,64,512]{2,1,0:T(8,128)(2,1)S(1)}, bf16[4,64,512]{2,1,0:T(8,128)(2,1)}, u32[]{:S(2)}) copy-start(bf16[4,64,512]{2,1,0:T(8,128)(2,1)} %param.17) | copy-start | bytes 786436
  29.6 2.0 %copy-start.5 = (f32[512]{0:T(512)S(1)}, f32[512]{0:T(512)}, u32[]{:S(2)}) copy-start(f32[512]{0:T(512)} %param.15) | copy-start | bytes 6148
  29.6 2.0 %copy-start.8 = (f32[512]{0:T(512)S(1)}, f32[512]{0:T(512)}, u32[]{:S(2)}) copy-start(f32[512]{0:T(512)} %param.16) | copy-start | bytes 6148
  31.3 3.6 %copy-start.2 = (bf16[256,1024]{1,0:T(8,128)(2,1)S(1)}, bf16[256,1024]{1,0:T(8,128)(2,1)}, u32[]{:S(2)}) copy-start(bf16[256,1024]{1,0:T(8,128)(2,1)} %concatenate.27) | copy-start | bytes 1572868
  34.1 0.8 copy-start.1
  83.1 5.4 %copy-start.3 = (f32[384,512]{1,0:T(8,128)S(1)}, f32[384,512]{1,0:T(8,128)}, u32[]{:S(2)}) copy-start(f32[384,512]{1,0:T(8,128)} %reduce-scatter.2.cloned.1.call-done) | copy-start | bytes 2359300
  83.1 5.4 %collective-permute-start.3 = (f32[384,512]{1,0:T(8,128)}, f32[384,512]{1,0:T(8,128)S(1)}, u32[]{:S(2)}, u32[]{:S(2)}) collective-permute-start(f32[384,512]{1,0:T(8,128)} %reduce-scatter.2.cloned.1.call-done), channel_id=1, source_target_pairs={{0,4},{4,0},{8,12},{12,8},{16,20},{20,16},{24,28},{28,24},{1,5},{5... | collective-permute-start | bytes 2359304 | tf_op jit(solution)/shard_map/ppermute | solution.py:128
  85.0 11.9 %collective-permute-start.2 = (f32[4,1,512]{2,1,0:T(1,128)S(1)}, f32[4,1,512]{2,1,0:T(1,128)S(1)}, u32[]{:S(2)}, u32[]{:S(2)}) collective-permute-start(f32[4,1,512]{2,1,0:T(1,128)S(1)} %slice.52), channel_id=1, source_target_pairs={{0,1},{1,2},{2,3},{4,5},{5,6},{6,7},{8,9},{9,10},{10,11},{12,13},{... | collective-permute-start | bytes 24584 | tf_op jit(solution)/shard_map/ppermute | solution.py:14
  88.7 19.8 %collective-permute-start.4 = (f32[384,512]{1,0:T(8,128)S(1)}, f32[384,512]{1,0:T(8,128)}, u32[]{:S(2)}, u32[]{:S(2)}) collective-permute-start(f32[384,512]{1,0:T(8,128)S(1)} %add.112), channel_id=1, source_target_pairs={{0,8},{4,12},{8,0},{12,4},{16,24},{20,28},{24,16},{28,20},{1,9},{5... | collective-permute-start | bytes 2359304 | tf_op jit(solution)/shard_map/ppermute | solution.py:128
  110.6 58.4 %collective-permute-start.5 = (f32[384,512]{1,0:T(8,128)}, f32[384,512]{1,0:T(8,128)S(1)}, u32[]{:S(2)}, u32[]{:S(2)}) collective-permute-start(f32[384,512]{1,0:T(8,128)} %add.113), channel_id=1, source_target_pairs={{0,16},{4,20},{8,24},{12,28},{16,0},{20,4},{24,8},{28,12},{1,17},{... | collective-permute-start | bytes 2359304 | tf_op jit(solution)/shard_map/ppermute | solution.py:128
Sparse Core Ops, SparseCore 0:
  37.5 45.6 reduce-scatter.1
